TPU v7x, 32 devices: a whole 2x2x4 slice. The times are simulated.
32 devices in a mesh: ia: 4 (over z), ja: 4 (over y, x), ka: 2 (over core).
Axes of the slice: x: 2, y: 2, z: 4, core: 2. Of those that a mesh axis runs over, the one named last changes fastest.
Arguments:
- blocks: bfloat16 [4, 4, 4, 128, 128, 128], P('ia', 'ja', 'ka'), may hold values from -6 to 6
- coordinates: int32 [3, 4, 4, 4], P(None, 'ia', 'ja', 'ka'), may hold values from 0 to 3, as said below
- occupancy: int32 [4, 4, 4], P('ia', 'ja', 'ka'), may hold values from 0 to 1, as said below
- second_factor: bfloat16 [4, 512, 1024], P('ja', ('ia', 'ka')), may hold values from -12 to 12
- third_factor: bfloat16 [2, 512, 1024], P('ka', ('ia', 'ja')), may hold values from -0.0234375 to 0.0234375
- inverse_first: bfloat16 [1024, 1024], replicated
- inverse_second: bfloat16 [1024, 1024], replicated
Outputs:
- first_new: bfloat16 [4, 512, 1024], P('ia', ('ja', 'ka'))
- second_new: bfloat16 [4, 512, 1024], P('ja', ('ia', 'ka'))
Inputs may be any that keep to these rules, and one draw needn't show every extreme that they name: `occupancy`: each device has two slots; its second slot is occupied only where its first is. A device with two blocks is followed along ka, cyclically, by a device with none. Some device holds two blocks. coordinates[0], [1], [2] of a slot are a block row among 4, a block row among 4 and a block layer among 4 of its device's ranges; the two slots of a device name different layers.
All inputs are finite; a program needn't handle non-finite values.
Results may differ from a plain program's by a relative error of at most 0.006.
Values may be sent and summed in bfloat16 or wider, within the bound.
A program may use at most 128 MiB of HBM per device.

v0:
```python
import jax
import jax.numpy as jnp
from jax import lax
from jax.sharding import PartitionSpec as P

IB = 4
JB = 4


def passed_along(block, axis, distance):
    devices = range(lax.axis_size(axis))
    route = [((i - distance) % len(devices), i) for i in devices]
    return lax.ppermute(block, axis, route)


def block_products(tensor_block, left_rows, layer_slab, contract):
    block_edge = tensor_block.shape[0]
    step_rows = max(block_edge // 4, 1)
    summed = jnp.zeros((block_edge, left_rows.shape[1]), jnp.float32)
    for first_row in range(0, block_edge, step_rows):
        khatri = left_rows[first_row : first_row + step_rows][:, None, :] * layer_slab[None, :, :]
        if contract == 1:
            block_part = tensor_block[:, first_row : first_row + step_rows, :]
            contraction = (((1, 2), (0, 1)), ((), ()))
        else:
            block_part = tensor_block[first_row : first_row + step_rows]
            contraction = (((0, 2), (0, 1)), ((), ()))
        summed = summed + lax.dot_general(
            block_part, khatri, contraction, preferred_element_type=jnp.float32
        )
    return summed


def place_rows(partial_value, addend, block_index):
    block_edge = addend.shape[0]
    row_start = block_index * block_edge
    current = lax.dynamic_slice_in_dim(partial_value, row_start, block_edge, 0)
    return lax.dynamic_update_slice_in_dim(partial_value, addend, row_start, 0)


def pick_rows(source, block_index, block_edge):
    return lax.dynamic_slice_in_dim(source, block_index * block_edge, block_edge, 0)


def body(
    blocks, coordinates, occupancy, second_factor, third_factor, inverse_first, inverse_second
):
    block_edge = blocks.shape[-1]
    rank_width = inverse_first.shape[0]
    own_blocks = blocks.reshape(2, block_edge, block_edge, block_edge)
    places = coordinates.reshape(3, 2)
    occupied = occupancy.reshape(2)
    second_rows = lax.all_gather(second_factor, ("ia", "ka"), axis=1, tiled=True)[0]
    layer_rows = lax.all_gather(third_factor, ("ia", "ja"), axis=1, tiled=True)[0]
    slot_meta = jnp.stack([occupied[1], places[0, 1], places[1, 1]]).astype(jnp.bfloat16)
    arrived, arrived_layer, arrived_meta = passed_along(
        (own_blocks[1], pick_rows(layer_rows, places[2, 1], block_edge), slot_meta), "ka", 1
    )
    arrived_index = arrived_meta.astype(jnp.int32)
    keep_own = occupied[0] > 0
    tensor_block = jnp.where(keep_own, own_blocks[0], arrived)
    layer_slab = jnp.where(keep_own, pick_rows(layer_rows, places[2, 0], block_edge), arrived_layer)
    row_block = jnp.where(keep_own, places[0, 0], arrived_index[1])
    col_block = jnp.where(keep_own, places[1, 0], arrived_index[2])
    weight = jnp.where(keep_own, 1, arrived_index[0]).astype(jnp.float32)
    first_partial = jnp.zeros((IB * block_edge, rank_width), jnp.float32)
    contribution = block_products(
        tensor_block, pick_rows(second_rows, col_block, block_edge), layer_slab, 1
    )
    first_partial = place_rows(first_partial, contribution * weight, row_block)
    summed_rows = lax.psum(first_partial, ("ja", "ka"))
    first_rows = jnp.dot(
        summed_rows.astype(jnp.bfloat16), inverse_first, preferred_element_type=jnp.float32
    ).astype(jnp.bfloat16)
    share_rows = first_rows.shape[0] // lax.axis_size(("ja", "ka"))
    first_new = lax.dynamic_slice_in_dim(
        first_rows, lax.axis_index(("ja", "ka")) * share_rows, share_rows, 0
    )
    second_partial = jnp.zeros((JB * block_edge, rank_width), jnp.float32)
    contribution = block_products(
        tensor_block, pick_rows(first_rows, row_block, block_edge), layer_slab, 0
    )
    second_partial = place_rows(second_partial, contribution * weight, col_block)
    owned_second = lax.psum_scatter(
        second_partial[None], ("ia", "ka"), scatter_dimension=1, tiled=True
    )[0]
    second_new = jnp.dot(
        owned_second.astype(jnp.bfloat16), inverse_second, preferred_element_type=jnp.float32
    ).astype(jnp.bfloat16)
    return (first_new[None], second_new[None])


def solution(mesh):
    in_specs = (
        P("ia", "ja", "ka", None, None, None),
        P(None, "ia", "ja", "ka"),
        P("ia", "ja", "ka"),
        P("ja", ("ia", "ka"), None),
        P("ka", ("ia", "ja"), None),
        P(),
        P(),
    )
    out_specs = (P("ia", ("ja", "ka"), None), P("ja", ("ia", "ka"), None))
    return jax.shard_map(body, mesh=mesh, in_specs=in_specs, out_specs=out_specs, check_vma=False)
```

profile of v0, /device:TPU:0, one launch (start us, length us, event | category | flops | bytes accessed | tf_op | source)
XLA Modules:
  0.0 221.0 jit_solution(3574953310530504106)
XLA Ops:
  7.2 0.0 copy-start
  7.2 0.0 copy-start.5
  7.2 0.0 copy-start.4
  7.2 0.0 all-gather.5.cloned.1.call-start
  7.2 4.9 %slice_bitcast_fusion = bf16[128,128,128]{2,1,0:T(8,128)(2,1)} fusion(bf16[1,1,2,128,128,128]{5,4,3,2,1,0:T(8,128)(2,1)} %param.7), kind=kLoop, calls=%fused_computation.33 | loop fusion | bytes 8388608 | tf_op jit(solution)/shard_map/squeeze | solution.py:57
  12.1 0.5 collective-permute-start
  12.6 0.0 all-gather.5.cloned.1.call-update
  12.6 0.0 all-gather.3.cloned.1.call-start
  12.7 0.7 all-gather.3.cloned.1.call-update
  13.4 0.0 reduce-scatter.2.cloned.1.call-start
  13.4 0.0 copy-done.5
  13.5 0.6 slice.105
  14.1 0.0 copy-done.4
  14.1 0.6 fusion.98
  15.4 0.7 fusion.100
  16.0 54.2 %all-gather.5.cloned.1.call-done = bf16[1,512,1024]{2,1,0:T(8,128)(2,1)} async-done(((bf16[1,32,1024]{2,1,0:T(8,128)(2,1)}), bf16[1,512,1024]{2,1,0:T(8,128)(2,1)}) %all-gather.5.cloned.1.call-update) | async-done | bytes 1048592 | tf_op jit(solution)/shard_map/all_gather | solution.py:54
  70.3 1.0 dynamic-slice_bitcast_fusion
  71.2 0.1 collective-permute-start.2
  71.3 2.0 pad_maximum_fusion
  73.4 0.5 collective-permute-start.1
  74.5 0.1 collective-permute-done.1
  74.7 0.7 fusion.99
  78.5 14.5 %all-gather.3.cloned.1.call-done = bf16[1,512,1024]{2,1,0:T(8,128)(2,1)} async-done(((bf16[1,64,1024]{2,1,0:T(8,128)(2,1)}), bf16[1,512,1024]{2,1,0:T(8,128)(2,1)}) %all-gather.3.cloned.1.call-update) | async-done | bytes 1048592 | tf_op jit(solution)/shard_map/all_gather | solution.py:53
  93.0 1.0 dynamic-slice_bitcast_fusion.5
  93.9 0.0 collective-permute-done.2
  93.9 1.0 bitcast_select_fusion.1
  95.0 0.0 collective-permute-done
  95.0 3.9 %bitcast_select_fusion = bf16[128,128,128]{2,1,0:T(8,128)(2,1)S(1)} fusion(bf16[128,128,128]{2,1,0:T(8,128)(2,1)} %collective-permute-done, bf16[1,1,2,128,128,128]{5,4,3,2,1,0:T(8,128)(2,1)} %param.7, pred[]{:T(512)} %bitcast), kind=kLoop, calls=%fused_computation.16 | loop fusion | flops 2097152 | bytes 12582913 | tf_op jit(solution)/shard_map/jit(_where)/select_n | solution.py:61
  98.9 0.0 copy-start.1
  98.9 0.8 fusion.97
  99.7 1.3 fusion.47
  101.0 0.0 copy-done.1
  101.0 1.3 fusion.50
  102.3 1.3 fusion.53
  103.7 1.6 broadcast.9
  105.3 2.1 fusion.86
  107.4 57.5 %all-reduce.1 = bf16[512,1024]{1,0:T(8,128)(2,1)S(1)} all-reduce(f32[512,1024]{1,0:T(8,128)} %fusion.86), channel_id=1, replica_groups=mesh['ia'=4,'ja'=4,'ka'=2] {'ja','ka'}, use_global_device_ids=true, to_apply=%region_0.1 | all-reduce | flops 524288 | bytes 3145728 | tf_op jit(solution)/shard_map/psum | solution.py:71
  164.9 0.0 copy-done
  164.9 1.3 convolution_convert_fusion
  166.2 0.0 copy-start.3
  166.2 1.0 copy-done.3
  167.2 0.0 copy-start.2
  167.2 2.6 %fusion.35 = f32[128,1024]{1,0:T(8,128)S(1)} fusion(bf16[128,128,128]{2,1,0:T(8,128)(2,1)} %copy-done.1, bf16[32,1024]{1,0:T(8,128)(2,1)S(1)} %get-tuple-element.8, bf16[128,1024]{1,0:T(8,128)(2,1)S(1)} %bitcast_select_fusion.1), kind=kOutput, calls=%fused_computation.36 | convolution fusion | flops 1090519040 | bytes 5046272 | tf_op jit(solution)/shard_map/dot_general | solution.py:28
  169.8 0.0 copy-done.2
  169.8 1.3 fusion.38
  171.2 1.3 fusion.41
  172.5 1.6 broadcast_in_dim.9
  174.1 2.3 %fusion.77 = f32[1,512,1024]{2,1,0:T(8,128)} fusion(f32[1,512,1024]{2,1,0:T(8,128)} %broadcast_in_dim.9, s32[]{:T(128)S(6)} %select_n.47, f32[128,1024]{1,0:T(8,128)S(1)} %fusion.41, f32[128,1024]{1,0:T(8,128)S(1)} %fusion.38, f32[128,1024]{1,0:T(8,128)S(1)} %fusion.35, bf16[128,128,128]{2,1,0:T(8,128)(2,1)S(1)} %copy-done.2, ...), kind=kOutput, calls=%fused_computation.50 | convolution fusion | flops 1091043328 | bytes 6619144 | tf_op jit(solution)/shard_map/dot_general | solution.py:28
  176.4 0.0 reduce-scatter.2.cloned.1.call-update
  176.5 1.6 dynamic-slice_bitcast_fusion.1
  178.0 33.6 %reduce-scatter.2.cloned.1.call-done = f32[1,64,1024]{2,1,0:T(8,128)} async-done(((f32[1,512,1024]{2,1,0:T(8,128)}), f32[1,64,1024]{2,1,0:T(8,128)}) %reduce-scatter.2.cloned.1.call-update) | async-done | bytes 262160 | tf_op jit(solution)/shard_map/reduce_scatter | solution.py:84
  211.6 2.8 %fusion.89 = bf16[1,64,1024]{2,1,0:T(8,128)(2,1)} fusion(bf16[1024,1024]{1,0:T(8,128)(2,1)} %param.13, f32[1,64,1024]{2,1,0:T(8,128)} %reduce-scatter.2.cloned.1.call-done), kind=kOutput, calls=%fused_computation.55 | convolution fusion | flops 134348800 | bytes 2490368 | tf_op jit(solution)/shard_map/dot_general | solution.py:87
  (4 shorter events, 0.0 us)
Async XLA Ops:
  7.2 157.8 %copy-start = (bf16[1024,1024]{1,0:T(8,128)(2,1)S(1)}, bf16[1024,1024]{1,0:T(8,128)(2,1)}, u32[]{:S(2)}) copy-start(bf16[1024,1024]{1,0:T(8,128)(2,1)} %param.12) | copy-start | bytes 6291460
  7.2 6.3 %copy-start.5 = (s32[1,1,2]{2,1,0:T(1,128)S(1)}, s32[1,1,2]{2,1,0:T(1,128)}, u32[]{:S(2)}) copy-start(s32[1,1,2]{2,1,0:T(1,128)} %param.9) | copy-start | bytes 28
  7.2 6.9 %copy-start.4 = (s32[3,1,1,2]{0,3,2,1:T(2,128)S(1)}, s32[3,1,1,2]{0,3,2,1:T(2,128)}, u32[]{:S(2)}) copy-start(s32[3,1,1,2]{0,3,2,1:T(2,128)} %param.8) | copy-start | bytes 76
  7.2 63.1 %all-gather.5.cloned.1.call-start = ((), (), s32[]{:S(2)}) async-start(), calls=%async_computation.2 | async-start | bytes 1114112 | tf_op jit(solution)/shard_map/all_gather | solution.py:54
  12.1 82.9 %collective-permute-start = (bf16[128,128,128]{2,1,0:T(8,128)(2,1)}, bf16[128,128,128]{2,1,0:T(8,128)(2,1)}, u32[]{:S(2)}, u32[]{:S(2)}) collective-permute-start(bf16[128,128,128]{2,1,0:T(8,128)(2,1)} %slice_bitcast_fusion), channel_id=1, source_target_pairs={{1,0},{0,1},{3,2},{2,3},{5,4},{4,5},{7,6},{6,7},{9,8},{8,9},{11,10... | collective-permute-start | bytes 12582920 | tf_op jit(solution)/shard_map/ppermute | solution.py:13
  12.6 80.3 %all-gather.3.cloned.1.call-start = ((), (), s32[]{:S(2)}) async-start(), calls=%async_computation.1 | async-start | bytes 1179648 | tf_op jit(solution)/shard_map/all_gather | solution.py:53
  13.4 198.3 %reduce-scatter.2.cloned.1.call-start = ((), (), s32[]{:S(2)}) async-start(), calls=%async_computation.3 | async-start | bytes 2359296 | tf_op jit(solution)/shard_map/reduce_scatter | solution.py:84
  71.2 22.7 %collective-permute-start.2 = (bf16[128,1024]{1,0:T(8,128)(2,1)S(1)}, bf16[128,1024]{1,0:T(8,128)(2,1)S(1)}, u32[]{:S(2)}, u32[]{:S(2)}) collective-permute-start(bf16[128,1024]{1,0:T(8,128)(2,1)S(1)} %dynamic-slice_bitcast_fusion), channel_id=1, source_target_pairs={{1,0},{0,1},{3,2},{2,3},{5,4},{4,5},{7,6},{6,7},{9,8},{8,9},{11,10... | collective-permute-start | bytes 786440 | tf_op jit(solution)/shard_map/ppermute | solution.py:13
  73.4 1.3 collective-permute-start.1
  98.9 2.1 copy-start.1
  166.2 1.0 copy-start.3
  167.2 2.7 %copy-start.2 = (bf16[128,128,128]{2,1,0:T(8,128)(2,1)S(1)}, bf16[128,128,128]{2,1,0:T(8,128)(2,1)}, u32[]{:S(2)}) copy-start(bf16[128,128,128]{2,1,0:T(8,128)(2,1)} %copy-done.1) | copy-start | bytes 12582916
Sparse Core Ops, SparseCore 0:
  12.8 57.4 all-gather.4
  71.9 21.0 all-gather.2
  176.6 35.0 reduce-scatter.1
where the time goes:
time: 221 us
  waiting for transfers between devices  103 us (47%)
  blocking collectives  57.5 us (26%)
  between operations  18.5 us (8%)
  matrix products  17.8 us (8%)
  local copies, waits for them, and re-layouts  16 us (7%)
  other arithmetic  6.99 us (3%)
    psum x1, blocking collectives, body(): summed_rows = lax.psum(first_partial, ('ja', 'ka'))  57.5 us
    all_gather x1, waiting for transfers between devices, body(): lax.all_gather(third_factor, ('ia', 'ja'), axis=1, tiled=True)[0]  54.2 us
    reduce_scatter x1, waiting for transfers between devices, body(): lax.psum_scatter(second_partial[None], ('ia', 'ka'), scatter_dimension=1,...  33.6 us
    all_gather x1, waiting for transfers between devices, body(): lax.all_gather(second_factor, ('ia', 'ka'), axis=1, tiled=True)[0]  14.5 us
    dot_general x8, matrix products, block_products(): lax.dot_general(block_part, khatri, contraction, preferred_element_type=j...  13.7 us
    squeeze x1, local copies, waits for them, and re-layouts, body(): own_blocks[1]  4.87 us
  transfers between devices with their start and end apart: 6, of which 4 were waited for; matrix products, arithmetic and copies ran while one was open for 4% of the time, Pallas kernels for 0%

commit v1 on v0

--- a/solution.py
+++ b/solution.py
@@ -5,6 +5,27 @@
 
 IB = 4
 JB = 4
+
+
+def gather_around(shard, axis, dim):
+    devices, place, rows = (lax.axis_size(axis), lax.axis_index(axis), shard.shape[dim])
+    forward = [(i, (i + 1) % devices) for i in range(devices)]
+    left = [(i, (i - 1) % devices) for i in range(devices)]
+    result = jnp.zeros((*shard.shape[:dim], devices * rows, *shard.shape[dim + 1 :]), shard.dtype)
+    result = lax.dynamic_update_slice_in_dim(result, shard, place * rows, axis=dim)
+    from_left = from_right = shard
+    half = devices // 2
+    for step in range(1, half + 1):
+        from_left = lax.ppermute(from_left, axis, forward)
+        result = lax.dynamic_update_slice_in_dim(
+            result, from_left, (place - step) % devices * rows, axis=dim
+        )
+        if step < devices - half:
+            from_right = lax.ppermute(from_right, axis, left)
+            result = lax.dynamic_update_slice_in_dim(
+                result, from_right, (place + step) % devices * rows, axis=dim
+            )
+    return result
 
 
 def passed_along(block, axis, distance):
@@ -50,7 +71,7 @@
     own_blocks = blocks.reshape(2, block_edge, block_edge, block_edge)
     places = coordinates.reshape(3, 2)
     occupied = occupancy.reshape(2)
-    second_rows = lax.all_gather(second_factor, ("ia", "ka"), axis=1, tiled=True)[0]
+    second_rows = gather_around(second_factor, ("ia", "ka"), 1)[0]
     layer_rows = lax.all_gather(third_factor, ("ia", "ja"), axis=1, tiled=True)[0]
     slot_meta = jnp.stack([occupied[1], places[0, 1], places[1, 1]]).astype(jnp.bfloat16)
     arrived, arrived_layer, arrived_meta = passed_along(

time: 221 us -> 202 us (0.914)
  waiting for transfers between devices: 103 us -> 71.9 us
  starting transfers between devices: 1.18 us -> 12.5 us
    all_gather x1, waiting for transfers between devices: 54.2 us -> 31.1 us  [body(): lax.all_gather(third_factor, ('ia', 'ja'), axis=1, tiled=True)[0]]
    all_gather x1 -> x0, waiting for transfers between devices: 14.5 us -> none  [body(): lax.all_gather(second_factor, ('ia', 'ka'), axis=1, tiled=True)[0]]
    ppermute x0 -> x7, starting transfers between devices: none -> 11.8 us  [the longest x3 11.3 us: gather_around(): from_right = lax.ppermute(from_right, axis, left)]
    ppermute x0 -> x7, waiting for transfers between devices: none -> 7.02 us  [the longest x4 7.01 us: gather_around(): from_left = lax.ppermute(from_left, axis, forward)]
  transfers between devices with their start and end apart: 6 -> 12, of which waited for: 4 -> 5; matrix products, arithmetic and copies ran while one was open for 4% -> 4% of each run, Pallas kernels for 0% -> 0%
where the time goes in v1:
time: 202 us; the launch traced here: 201 us
  waiting for transfers between devices  71.9 us (36%)
  blocking collectives  58 us (29%)
  between operations  18.9 us (9%)
  matrix products  17.8 us (9%)
  local copies, waits for them, and re-layouts  15.1 us (7%)
  starting transfers between devices  12.5 us (6%)
  other arithmetic  6.89 us (3%)
    psum x1, blocking collectives, body(): summed_rows = lax.psum(first_partial, ('ja', 'ka'))  58 us
    reduce_scatter x1, waiting for transfers between devices, body(): lax.psum_scatter(second_partial[None], ('ia', 'ka'), scatter_dimension=1,...  32.4 us
    all_gather x1, waiting for transfers between devices, body(): lax.all_gather(third_factor, ('ia', 'ja'), axis=1, tiled=True)[0]  31.1 us
    dot_general x8, matrix products, block_products(): lax.dot_general(block_part, khatri, contraction, preferred_element_type=j...  13.7 us
    ppermute x3, starting transfers between devices, gather_around(): from_right = lax.ppermute(from_right, axis, left)  11.3 us
    ppermute x4, waiting for transfers between devices, gather_around(): from_left = lax.ppermute(from_left, axis, forward)  7.01 us
    squeeze x1, local copies, waits for them, and re-layouts, body(): own_blocks[1]  4.85 us
  transfers between devices with their start and end apart: 12, of which 5 were waited for; matrix products, arithmetic and copies ran while one was open for 4% of the time, Pallas kernels for 0%

profile of v1, /device:TPU:0, one launch (start us, length us, event | category | flops | bytes accessed | tf_op | source)
XLA Modules:
  0.0 201.2 jit_solution(318100358102554711)
XLA Ops:
  7.2 0.0 copy-start
  7.2 0.0 copy-start.4
  7.2 0.0 copy-start.5
  7.2 0.0 copy-start.6
  7.2 0.0 all-gather.2.cloned.1.call-start
  7.3 4.9 %slice_bitcast_fusion = bf16[128,128,128]{2,1,0:T(8,128)(2,1)} fusion(bf16[1,1,2,128,128,128]{5,4,3,2,1,0:T(8,128)(2,1)} %param.7), kind=kLoop, calls=%fused_computation.33 | loop fusion | bytes 8388608 | tf_op jit(solution)/shard_map/squeeze | solution.py:78
  12.1 0.5 collective-permute-start
  12.6 0.0 copy-done.4
  12.6 0.0 collective-permute-start.1
  12.6 4.7 %collective-permute-start.2 = (bf16[1,64,1024]{2,1,0:T(8,128)(2,1)S(1)}, bf16[1,64,1024]{2,1,0:T(8,128)(2,1)S(1)}, u32[]{:S(2)}, u32[]{:S(2)}) collective-permute-start(bf16[1,64,1024]{2,1,0:T(8,128)(2,1)S(1)} %copy-done.4), channel_id=1, source_target_pairs={{0,25},{1,0},{8,1},{9,8},{16,9},{17,16},{24,17},{25,24},{2,27},{3,... | collective-permute-start | bytes 393224 | tf_op jit(solution)/shard_map/ppermute | solution.py:24
  17.3 0.0 all-gather.2.cloned.1.call-update
  17.3 0.0 reduce-scatter.2.cloned.1.call-start
  17.4 0.0 copy-done.5
  17.4 0.6 fusion.100
  18.0 0.0 copy-done.6
  18.0 0.6 slice.101
  18.6 1.9 pad_maximum_fusion
  20.5 0.0 collective-permute-start.8
  20.6 0.1 squeeze.47
  20.7 0.6 fusion.98
  22.7 0.0 collective-permute-done.8
  22.7 0.7 fusion.99
  26.6 0.0 collective-permute-done.1
  26.6 0.5 collective-permute-start.3
  27.1 0.0 collective-permute-done.2
  27.1 3.1 %collective-permute-start.4 = (bf16[1,64,1024]{2,1,0:T(8,128)(2,1)S(1)}, bf16[1,64,1024]{2,1,0:T(8,128)(2,1)S(1)}, u32[]{:S(2)}, u32[]{:S(2)}) collective-permute-start(bf16[1,64,1024]{2,1,0:T(8,128)(2,1)S(1)} %collective-permute-done.2), channel_id=1, source_target_pairs={{0,25},{1,0},{8,1},{9,8},{16,9},{17,16},{24,17},{25,24},{2,27},{3,... | collective-permute-start | bytes 393224 | tf_op jit(solution)/shard_map/ppermute | solution.py:24
  30.2 3.8 %collective-permute-done.3 = bf16[1,64,1024]{2,1,0:T(8,128)(2,1)S(1)} collective-permute-done((bf16[1,64,1024]{2,1,0:T(8,128)(2,1)S(1)}, bf16[1,64,1024]{2,1,0:T(8,128)(2,1)S(1)}, u32[]{:S(2)}, u32[]{:S(2)}) %collective-permute-start.3) | collective-permute-done | bytes 131104 | tf_op jit(solution)/shard_map/ppermute | solution.py:19
  34.0 0.0 collective-permute-start.5
  34.0 0.0 collective-permute-done.4
  34.0 3.5 %collective-permute-start.6 = (bf16[1,64,1024]{2,1,0:T(8,128)(2,1)S(1)}, bf16[1,64,1024]{2,1,0:T(8,128)(2,1)S(1)}, u32[]{:S(2)}, u32[]{:S(2)}) collective-permute-start(bf16[1,64,1024]{2,1,0:T(8,128)(2,1)S(1)} %collective-permute-done.4), channel_id=1, source_target_pairs={{0,25},{1,0},{8,1},{9,8},{16,9},{17,16},{24,17},{25,24},{2,27},{3,... | collective-permute-start | bytes 393224 | tf_op jit(solution)/shard_map/ppermute | solution.py:24
  37.6 3.2 %collective-permute-done.5 = bf16[1,64,1024]{2,1,0:T(8,128)(2,1)S(1)} collective-permute-done((bf16[1,64,1024]{2,1,0:T(8,128)(2,1)S(1)}, bf16[1,64,1024]{2,1,0:T(8,128)(2,1)S(1)}, u32[]{:S(2)}, u32[]{:S(2)}) %collective-permute-start.5) | collective-permute-done | bytes 131104 | tf_op jit(solution)/shard_map/ppermute | solution.py:19
  40.8 0.0 collective-permute-start.7
  40.8 0.0 collective-permute-done.6
  40.9 31.1 %all-gather.2.cloned.1.call-done = bf16[1,512,1024]{2,1,0:T(8,128)(2,1)} async-done(((bf16[1,32,1024]{2,1,0:T(8,128)(2,1)}), bf16[1,512,1024]{2,1,0:T(8,128)(2,1)}) %all-gather.2.cloned.1.call-update) | async-done | bytes 1048592 | tf_op jit(solution)/shard_map/all_gather | solution.py:75
  71.9 1.0 dynamic-slice_bitcast_fusion
  72.9 0.1 collective-permute-start.9
  73.0 0.0 collective-permute-done.7
  73.1 1.4 collective-permute-done.9
  74.5 1.0 bitcast_select_fusion.1
  75.5 0.0 collective-permute-done
  75.5 3.9 %bitcast_select_fusion = bf16[128,128,128]{2,1,0:T(8,128)(2,1)S(1)} fusion(bf16[128,128,128]{2,1,0:T(8,128)(2,1)} %collective-permute-done, bf16[1,1,2,128,128,128]{5,4,3,2,1,0:T(8,128)(2,1)} %param.7, pred[]{:T(512)} %bitcast), kind=kLoop, calls=%fused_computation.16 | loop fusion | flops 2097152 | bytes 12582913 | tf_op jit(solution)/shard_map/jit(_where)/select_n | solution.py:82
  79.5 0.0 copy-start.1
  79.5 0.8 fusion.97
  80.3 1.3 fusion.47
  81.6 0.0 copy-done.1
  81.6 1.3 fusion.50
  82.9 1.3 fusion.53
  84.2 1.6 broadcast.22
  85.8 2.1 %fusion.86 = f32[512,1024]{1,0:T(8,128)} fusion(f32[512,1024]{1,0:T(8,128)} %broadcast.22, s32[]{:T(128)S(6)} %select_n.123, f32[128,1024]{1,0:T(8,128)S(1)} %fusion.53, f32[128,1024]{1,0:T(8,128)S(1)} %fusion.50, f32[128,1024]{1,0:T(8,128)S(1)} %fusion.47, bf16[128,1024]{1,0:T(8,128)(2,1)S(1)} %bitcast_select_fusion.1, ...), kind=kOutput, calls=%fused_computation.53 | convolution fusion | flops 1078460416 | bytes 3473416 | tf_op jit(solution)/shard_map/dot_general | solution.py:49
  88.0 58.0 %all-reduce.1 = bf16[512,1024]{1,0:T(8,128)(2,1)S(1)} all-reduce(f32[512,1024]{1,0:T(8,128)} %fusion.86), channel_id=1, replica_groups=mesh['ia'=4,'ja'=4,'ka'=2] {'ja','ka'}, use_global_device_ids=true, to_apply=%region_0.1 | all-reduce | flops 524288 | bytes 3145728 | tf_op jit(solution)/shard_map/psum | solution.py:92
  146.0 0.0 copy-done
  146.0 1.3 convolution_convert_fusion
  147.3 0.0 copy-start.3
  147.3 1.0 copy-done.3
  148.3 2.6 %fusion.35 = f32[128,1024]{1,0:T(8,128)S(1)} fusion(bf16[128,128,128]{2,1,0:T(8,128)(2,1)} %copy-done.1, bf16[32,1024]{1,0:T(8,128)(2,1)S(1)} %get-tuple-element.8, bf16[128,1024]{1,0:T(8,128)(2,1)S(1)} %bitcast_select_fusion.1), kind=kOutput, calls=%fused_computation.36 | convolution fusion | flops 1090519040 | bytes 5046272 | tf_op jit(solution)/shard_map/dot_general | solution.py:49
  150.9 0.0 copy-done.2
  151.0 1.3 fusion.38
  152.3 1.3 fusion.41
  153.6 1.6 broadcast_in_dim.9
  155.2 2.3 %fusion.77 = f32[1,512,1024]{2,1,0:T(8,128)} fusion(f32[1,512,1024]{2,1,0:T(8,128)} %broadcast_in_dim.9, s32[]{:T(128)S(6)} %select_n.116, f32[128,1024]{1,0:T(8,128)S(1)} %fusion.41, f32[128,1024]{1,0:T(8,128)S(1)} %fusion.38, f32[128,1024]{1,0:T(8,128)S(1)} %fusion.35, bf16[128,128,128]{2,1,0:T(8,128)(2,1)S(1)} %copy-done.2, ...), kind=kOutput, calls=%fused_computation.50 | convolution fusion | flops 1091043328 | bytes 6619144 | tf_op jit(solution)/shard_map/dot_general | solution.py:49
  157.5 0.0 reduce-scatter.2.cloned.1.call-update
  157.6 1.6 dynamic-slice_bitcast_fusion.1
  159.1 32.4 %reduce-scatter.2.cloned.1.call-done = f32[1,64,1024]{2,1,0:T(8,128)} async-done(((f32[1,512,1024]{2,1,0:T(8,128)}), f32[1,64,1024]{2,1,0:T(8,128)}) %reduce-scatter.2.cloned.1.call-update) | async-done | bytes 262160 | tf_op jit(solution)/shard_map/reduce_scatter | solution.py:105
  191.5 2.8 %fusion.89 = bf16[1,64,1024]{2,1,0:T(8,128)(2,1)} fusion(bf16[1024,1024]{1,0:T(8,128)(2,1)} %param.13, f32[1,64,1024]{2,1,0:T(8,128)} %reduce-scatter.2.cloned.1.call-done), kind=kOutput, calls=%fused_computation.55 | convolution fusion | flops 134348800 | bytes 2490368 | tf_op jit(solution)/shard_map/dot_general | solution.py:108
  (14 shorter events, 0.2 us)
Async XLA Ops:
  7.2 138.9 %copy-start = (bf16[1024,1024]{1,0:T(8,128)(2,1)S(1)}, bf16[1024,1024]{1,0:T(8,128)(2,1)}, u32[]{:S(2)}) copy-start(bf16[1024,1024]{1,0:T(8,128)(2,1)} %param.12) | copy-start | bytes 6291460
  7.2 5.4 %copy-start.4 = (bf16[1,64,1024]{2,1,0:T(8,128)(2,1)S(1)}, bf16[1,64,1024]{2,1,0:T(8,128)(2,1)}, u32[]{:S(2)}) copy-start(bf16[1,64,1024]{2,1,0:T(8,128)(2,1)} %param.10) | copy-start | bytes 393220
  7.2 10.2 %copy-start.5 = (s32[3,1,1,2]{0,3,2,1:T(2,128)S(1)}, s32[3,1,1,2]{0,3,2,1:T(2,128)}, u32[]{:S(2)}) copy-start(s32[3,1,1,2]{0,3,2,1:T(2,128)} %param.8) | copy-start | bytes 76
  7.2 10.8 %copy-start.6 = (s32[1,1,2]{2,1,0:T(1,128)S(1)}, s32[1,1,2]{2,1,0:T(1,128)}, u32[]{:S(2)}) copy-start(s32[1,1,2]{2,1,0:T(1,128)} %param.9) | copy-start | bytes 28
  7.2 64.7 %all-gather.2.cloned.1.call-start = ((), (), s32[]{:S(2)}) async-start(), calls=%async_computation.1 | async-start | bytes 1114112 | tf_op jit(solution)/shard_map/all_gather | solution.py:75
  12.1 63.4 %collective-permute-start = (bf16[128,128,128]{2,1,0:T(8,128)(2,1)}, bf16[128,128,128]{2,1,0:T(8,128)(2,1)}, u32[]{:S(2)}, u32[]{:S(2)}) collective-permute-start(bf16[128,128,128]{2,1,0:T(8,128)(2,1)} %slice_bitcast_fusion), channel_id=1, source_target_pairs={{1,0},{0,1},{3,2},{2,3},{5,4},{4,5},{7,6},{6,7},{9,8},{8,9},{11,10... | collective-permute-start | bytes 12582920 | tf_op jit(solution)/shard_map/ppermute | solution.py:34
  12.6 14.0 %collective-permute-start.1 = (bf16[1,64,1024]{2,1,0:T(8,128)(2,1)S(1)}, bf16[1,64,1024]{2,1,0:T(8,128)(2,1)S(1)}, u32[]{:S(2)}, u32[]{:S(2)}) collective-permute-start(bf16[1,64,1024]{2,1,0:T(8,128)(2,1)S(1)} %copy-done.4), channel_id=1, source_target_pairs={{0,1},{1,8},{8,9},{9,16},{16,17},{17,24},{24,25},{25,0},{2,3},{3,1... | collective-permute-start | bytes 393224 | tf_op jit(solution)/shard_map/ppermute | solution.py:19
  12.6 14.5 %collective-permute-start.2 = (bf16[1,64,1024]{2,1,0:T(8,128)(2,1)S(1)}, bf16[1,64,1024]{2,1,0:T(8,128)(2,1)S(1)}, u32[]{:S(2)}, u32[]{:S(2)}) collective-permute-start(bf16[1,64,1024]{2,1,0:T(8,128)(2,1)S(1)} %copy-done.4), channel_id=1, source_target_pairs={{0,25},{1,0},{8,1},{9,8},{16,9},{17,16},{24,17},{25,24},{2,27},{3,... | collective-permute-start | bytes 393224 | tf_op jit(solution)/shard_map/ppermute | solution.py:24
  17.3 174.2 %reduce-scatter.2.cloned.1.call-start = ((), (), s32[]{:S(2)}) async-start(), calls=%async_computation.2 | async-start | bytes 2359296 | tf_op jit(solution)/shard_map/reduce_scatter | solution.py:105
  20.5 2.2 %collective-permute-start.8 = (bf16[3]{0:T(256)(128)(2,1)S(1)}, bf16[3]{0:T(256)(128)(2,1)S(1)}, u32[]{:S(2)}, u32[]{:S(2)}) collective-permute-start(bf16[3]{0:T(256)(128)(2,1)S(1)} %pad_maximum_fusion), channel_id=1, source_target_pairs={{1,0},{0,1},{3,2},{2,3},{5,4},{4,5},{7,6},{6,7},{9,8},{8,9},{11,10... | collective-permute-start | bytes 26 | tf_op jit(solution)/shard_map/ppermute | solution.py:34
  26.6 7.5 %collective-permute-start.3 = (bf16[1,64,1024]{2,1,0:T(8,128)(2,1)S(1)}, bf16[1,64,1024]{2,1,0:T(8,128)(2,1)S(1)}, u32[]{:S(2)}, u32[]{:S(2)}) collective-permute-start(bf16[1,64,1024]{2,1,0:T(8,128)(2,1)S(1)} %collective-permute-done.1), channel_id=1, source_target_pairs={{0,1},{1,8},{8,9},{9,16},{16,17},{17,24},{24,25},{25,0},{2,3},{3,1... | collective-permute-start | bytes 393224 | tf_op jit(solution)/shard_map/ppermute | solution.py:19
  27.1 6.9 %collective-permute-start.4 = (bf16[1,64,1024]{2,1,0:T(8,128)(2,1)S(1)}, bf16[1,64,1024]{2,1,0:T(8,128)(2,1)S(1)}, u32[]{:S(2)}, u32[]{:S(2)}) collective-permute-start(bf16[1,64,1024]{2,1,0:T(8,128)(2,1)S(1)} %collective-permute-done.2), channel_id=1, source_target_pairs={{0,25},{1,0},{8,1},{9,8},{16,9},{17,16},{24,17},{25,24},{2,27},{3,... | collective-permute-start | bytes 393224 | tf_op jit(solution)/shard_map/ppermute | solution.py:24
  34.0 6.8 %collective-permute-start.5 = (bf16[1,64,1024]{2,1,0:T(8,128)(2,1)S(1)}, bf16[1,64,1024]{2,1,0:T(8,128)(2,1)S(1)}, u32[]{:S(2)}, u32[]{:S(2)}) collective-permute-start(bf16[1,64,1024]{2,1,0:T(8,128)(2,1)S(1)} %collective-permute-done.3), channel_id=1, source_target_pairs={{0,1},{1,8},{8,9},{9,16},{16,17},{17,24},{24,25},{25,0},{2,3},{3,1... | collective-permute-start | bytes 393224 | tf_op jit(solution)/shard_map/ppermute | solution.py:19
  34.0 6.8 %collective-permute-start.6 = (bf16[1,64,1024]{2,1,0:T(8,128)(2,1)S(1)}, bf16[1,64,1024]{2,1,0:T(8,128)(2,1)S(1)}, u32[]{:S(2)}, u32[]{:S(2)}) collective-permute-start(bf16[1,64,1024]{2,1,0:T(8,128)(2,1)S(1)} %collective-permute-done.4), channel_id=1, source_target_pairs={{0,25},{1,0},{8,1},{9,8},{16,9},{17,16},{24,17},{25,24},{2,27},{3,... | collective-permute-start | bytes 393224 | tf_op jit(solution)/shard_map/ppermute | solution.py:24
  40.8 32.2 %collective-permute-start.7 = (bf16[1,64,1024]{2,1,0:T(8,128)(2,1)S(1)}, bf16[1,64,1024]{2,1,0:T(8,128)(2,1)S(1)}, u32[]{:S(2)}, u32[]{:S(2)}) collective-permute-start(bf16[1,64,1024]{2,1,0:T(8,128)(2,1)S(1)} %collective-permute-done.5), channel_id=1, source_target_pairs={{0,1},{1,8},{8,9},{9,16},{16,17},{17,24},{24,25},{25,0},{2,3},{3,1... | collective-permute-start | bytes 393224 | tf_op jit(solution)/shard_map/ppermute | solution.py:19
  72.9 1.6 collective-permute-start.9
  79.5 2.1 %copy-start.1 = (bf16[128,128,128]{2,1,0:T(8,128)(2,1)}, bf16[128,128,128]{2,1,0:T(8,128)(2,1)S(1)}, u32[]{:S(2)}) copy-start(bf16[128,128,128]{2,1,0:T(8,128)(2,1)S(1)} %bitcast_select_fusion) | copy-start | bytes 12582916
  147.3 1.0 copy-start.3
  148.3 2.7 %copy-start.2 = (bf16[128,128,128]{2,1,0:T(8,128)(2,1)S(1)}, bf16[128,128,128]{2,1,0:T(8,128)(2,1)}, u32[]{:S(2)}) copy-start(bf16[128,128,128]{2,1,0:T(8,128)(2,1)} %copy-done.1) | copy-start | bytes 12582916
Sparse Core Ops, SparseCore 0:
  17.5 54.4 all-gather.1
  157.7 33.7 reduce-scatter.1
